TPU v7x, 256 devices: a whole 4x4x8 slice. The times are simulated.
256 devices in a mesh: row: 8 (over x, core), col: 32 (over y, z).
Axes of the slice: x: 4, y: 4, z: 8, core: 2. Of those that a mesh axis runs over, the one named last changes fastest.
Arguments:
- upper_panel: float32 [2048, 8192], P('row', 'col')
- lower_panel: float32 [2048, 8192], P('row', 'col')
- pole_values: float32 [2, 8192], P(None, 'col'), may hold values from 0 to 4, as said below
- coupling: float32 [2, 8192], P(None, 'col'), may hold values from -6 to 6
- kept_mask: int32 [2, 8192], P(None, 'col'), may hold values from 0 to 1, as said below
- shifts: float32 [16384], P('col'), may hold values from 0 to 4
- source: int32 [16384], P('col'), may hold values from 0 to 16384, as said below
Outputs:
- vectors: float32 [2, 2048, 16384], P(None, 'row', 'col')
- slab_weight: float32 [16384], P('col')
Inputs may be any that keep to these rules, and one draw needn't show every extreme that they name: source[j] = 16384 marks an undeflated merged column; any other value is the pole whose child column the merged column copies, and no pole is named twice. Each device's 512 merged columns hold from 64 to 384 undeflated columns, and some device holds exactly 384. kept_mask is 0 exactly at the poles named in source. Some device of col holds no deflated pole: every pole of both children that it holds is kept. `pole_values`: every pole lies at least 0.4 / 16384 away from every entry of shifts.
All inputs are finite; a program needn't handle non-finite values.
Results may differ from a plain program's by a relative error of at most 0.0003.
Values sent between devices are 32-bit elements; how exact they have to be, the bound alone decides.
A program may use at most 64 MiB of HBM per device.

v0:
```python
import math
import jax
import jax.numpy as jnp
from jax import lax
from jax.sharding import PartitionSpec as P

N1 = 8192
exact_mode = lax.Precision.HIGHEST


def cauchy_block(pole_vals, weights, shift_vals):
    return weights[:, :, None] / (pole_vals[:, :, None] - shift_vals[None, None, :])


def local(upper_panel, lower_panel, pole_values, coupling, kept_mask, shifts, source):
    rows_here = upper_panel.shape[0]
    own_cols = shifts.shape[0]
    weighted = coupling * kept_mask.astype(jnp.float32)
    undeflated = source == 2 * N1
    child_base = jnp.array([0, N1], jnp.int32)
    zeros_acc = jnp.zeros((rows_here, own_cols), jnp.float32)
    pieces = (
        lax.all_gather(upper_panel, "col", axis=1, tiled=True),
        lax.all_gather(lower_panel, "col", axis=1, tiled=True),
        lax.all_gather(pole_values, "col", axis=1, tiled=True),
        lax.all_gather(weighted, "col", axis=1, tiled=True),
    )
    span_cols = math.gcd(pieces[0].shape[1], 1024)

    def advance(number, running):
        window = [
            lax.dynamic_slice_in_dim(member, number * span_cols, span_cols, 1) for member in pieces
        ]
        first_pole = number * span_cols
        cauchy = cauchy_block(window[2], window[3], shifts)
        indices = first_pole + lax.iota(jnp.int32, span_cols)
        one_hot = indices[None, :, None] + child_base[:, None, None] == source[None, None, :]
        basis_tile = jnp.where(undeflated[None, None, :], cauchy, one_hot.astype(jnp.float32))
        upper_acc = running[0] + jnp.dot(
            window[0], basis_tile[0], precision=exact_mode, preferred_element_type=jnp.float32
        )
        lower_acc = running[1] + jnp.dot(
            window[1], basis_tile[1], precision=exact_mode, preferred_element_type=jnp.float32
        )
        return (upper_acc, lower_acc, running[2] + jnp.sum(cauchy * cauchy, axis=(0, 1)))

    upper_acc, lower_acc, norm_sums = lax.fori_loop(
        0,
        pieces[0].shape[1] // span_cols,
        advance,
        (zeros_acc, zeros_acc, jnp.zeros((own_cols,), jnp.float32)),
    )
    scaling = jnp.where(undeflated, lax.rsqrt(norm_sums), 1.0)
    vectors = jnp.stack([upper_acc * scaling[None, :], lower_acc * scaling[None, :]])
    partial_weight = jnp.sum(vectors * vectors, axis=(0, 1))
    slab_weight = lax.psum(partial_weight, "row") / (2 * rows_here * lax.axis_size("row"))
    return (vectors, slab_weight)


def solution(mesh):
    in_specs = (
        P("row", "col"),
        P("row", "col"),
        P(None, "col"),
        P(None, "col"),
        P(None, "col"),
        P("col"),
        P("col"),
    )
    out_specs = (P(None, "row", "col"), P("col"))
    return jax.shard_map(local, mesh=mesh, in_specs=in_specs, out_specs=out_specs, check_vma=False)
```

profile of v0, /device:TPU:1, one launch (start us, length us, event | category | flops | bytes accessed | tf_op | source)
XLA Modules:
  0.0 310.2 jit_solution(16482954497444541827)
XLA Ops:
  7.2 0.0 all-gather.3.cloned.1.call-start
  7.2 0.7 all-gather.3.cloned.1.call-update
  7.9 0.0 all-gather.5.cloned.1.call-start
  7.9 0.7 all-gather.5.cloned.1.call-update
  8.7 0.7 convert_multiply_fusion
  9.4 41.5 %all_gather.13 = f32[2,8192]{1,0:T(2,128)S(1)} all-gather(f32[2,256]{1,0:T(2,128)S(1)} %convert_multiply_fusion), channel_id=1, replica_groups=mesh['row'=8,'col'=32] {'col'}, dimensions={1}, use_global_device_ids=true | all-gather | bytes 67584 | tf_op jit(solution)/shard_map/all_gather | solution.py:26
  50.9 39.2 %all_gather.14 = f32[2,8192]{1,0:T(2,128)S(1)} all-gather(f32[2,256]{1,0:T(2,128)} %param.12), channel_id=1, replica_groups=mesh['row'=8,'col'=32] {'col'}, dimensions={1}, use_global_device_ids=true | all-gather | bytes 67584 | tf_op jit(solution)/shard_map/all_gather | solution.py:25
  90.1 0.7 broadcast_compare_fusion
  90.8 23.1 %all-gather.3.cloned.1.call-done = f32[256,8192]{1,0:T(8,128)} async-done(((f32[256,256]{1,0:T(8,128)}), f32[256,8192]{1,0:T(8,128)}) %all-gather.3.cloned.1.call-update) | async-done | bytes 8388624 | tf_op jit(solution)/shard_map/all_gather | solution.py:23
  113.9 102.9 %all-gather.5.cloned.1.call-done = f32[256,8192]{1,0:T(8,128)} async-done(((f32[256,256]{1,0:T(8,128)}), f32[256,8192]{1,0:T(8,128)}) %all-gather.5.cloned.1.call-update) | async-done | bytes 8388624 | tf_op jit(solution)/shard_map/all_gather | solution.py:24
  216.8 68.3 %while.18 = (s32[]{:T(128)}, f32[256,512]{1,0:T(8,128)S(1)}, f32[256,512]{1,0:T(8,128)S(1)}, f32[512]{0:T(512)S(1)}, f32[256,8192]{1,0:T(8,128)}, /*index=5*/pre...) while((s32[]{:T(128)}, f32[256,512]{1,0:T(8,128)S(1)}, ...), condition=%wide.region_2.3_spmd.clone, body=%wide.region_0.2_spmd.clone.sunk | while | flops 3229093376 | bytes 12669679 | solution.py:47
  216.9 0.1 broadcast_add_fusion.2
  216.9 1.9 multiply_reduce_fusion.3
  218.8 3.3 %fusion.17 = f32[256,512]{1,0:T(8,128)S(1)} fusion(f32[2,1024,512]{2,1,0:T(8,128)S(1)} %get-tuple-element.347, f32[256,8192]{1,0:T(8,128)} %get-tuple-element.389, s32[]{:T(128)S(6)} %select_n.28, f32[256,512]{1,0:T(8,128)S(1)} %get-tuple-element.366, pred[]{:T(512)S(6)} %compare.3), kind=kOutput, calls=%fused_computation.9.clone.1 | convolution fusion | flops 1610874880 | bytes 4194309 | tf_op jit(solution)/shard_map/while/body/eval_jaxpr/dot_general | solution.py:42
  222.1 3.3 %fusion.16 = f32[256,512]{1,0:T(8,128)S(1)} fusion(f32[2,1024,512]{2,1,0:T(8,128)S(1)} %get-tuple-element.347, f32[256,8192]{1,0:T(8,128)} %get-tuple-element.383, s32[]{:T(128)S(6)} %select_n.28, f32[256,512]{1,0:T(8,128)S(1)} %get-tuple-element.365, pred[]{:T(512)S(6)} %compare.3), kind=kOutput, calls=%fused_computation.8.clone.1 | convolution fusion | flops 1610874880 | bytes 4194309 | tf_op jit(solution)/shard_map/while/body/eval_jaxpr/dot_general | solution.py:39
  225.4 0.1 broadcast_add_fusion.2
  225.5 1.9 multiply_reduce_fusion.3
  227.4 3.3 %fusion.17 = f32[256,512]{1,0:T(8,128)S(1)} fusion(f32[2,1024,512]{2,1,0:T(8,128)S(1)} %get-tuple-element.347, f32[256,8192]{1,0:T(8,128)} %get-tuple-element.389, s32[]{:T(128)S(6)} %select_n.28, f32[256,512]{1,0:T(8,128)S(1)} %get-tuple-element.366, pred[]{:T(512)S(6)} %compare.3), kind=kOutput, calls=%fused_computation.9.clone.1 | convolution fusion | flops 1610874880 | bytes 4194309 | tf_op jit(solution)/shard_map/while/body/eval_jaxpr/dot_general | solution.py:42
  230.6 3.3 %fusion.16 = f32[256,512]{1,0:T(8,128)S(1)} fusion(f32[2,1024,512]{2,1,0:T(8,128)S(1)} %get-tuple-element.347, f32[256,8192]{1,0:T(8,128)} %get-tuple-element.383, s32[]{:T(128)S(6)} %select_n.28, f32[256,512]{1,0:T(8,128)S(1)} %get-tuple-element.365, pred[]{:T(512)S(6)} %compare.3), kind=kOutput, calls=%fused_computation.8.clone.1 | convolution fusion | flops 1610874880 | bytes 4194309 | tf_op jit(solution)/shard_map/while/body/eval_jaxpr/dot_general | solution.py:39
  233.9 0.1 broadcast_add_fusion.2
  234.0 1.9 multiply_reduce_fusion.3
  235.9 3.3 %fusion.17 = f32[256,512]{1,0:T(8,128)S(1)} fusion(f32[2,1024,512]{2,1,0:T(8,128)S(1)} %get-tuple-element.347, f32[256,8192]{1,0:T(8,128)} %get-tuple-element.389, s32[]{:T(128)S(6)} %select_n.28, f32[256,512]{1,0:T(8,128)S(1)} %get-tuple-element.366, pred[]{:T(512)S(6)} %compare.3), kind=kOutput, calls=%fused_computation.9.clone.1 | convolution fusion | flops 1610874880 | bytes 4194309 | tf_op jit(solution)/shard_map/while/body/eval_jaxpr/dot_general | solution.py:42
  239.2 3.3 %fusion.16 = f32[256,512]{1,0:T(8,128)S(1)} fusion(f32[2,1024,512]{2,1,0:T(8,128)S(1)} %get-tuple-element.347, f32[256,8192]{1,0:T(8,128)} %get-tuple-element.383, s32[]{:T(128)S(6)} %select_n.28, f32[256,512]{1,0:T(8,128)S(1)} %get-tuple-element.365, pred[]{:T(512)S(6)} %compare.3), kind=kOutput, calls=%fused_computation.8.clone.1 | convolution fusion | flops 1610874880 | bytes 4194309 | tf_op jit(solution)/shard_map/while/body/eval_jaxpr/dot_general | solution.py:39
  242.5 0.1 broadcast_add_fusion.2
  242.6 1.9 multiply_reduce_fusion.3
  244.5 3.3 %fusion.17 = f32[256,512]{1,0:T(8,128)S(1)} fusion(f32[2,1024,512]{2,1,0:T(8,128)S(1)} %get-tuple-element.347, f32[256,8192]{1,0:T(8,128)} %get-tuple-element.389, s32[]{:T(128)S(6)} %select_n.28, f32[256,512]{1,0:T(8,128)S(1)} %get-tuple-element.366, pred[]{:T(512)S(6)} %compare.3), kind=kOutput, calls=%fused_computation.9.clone.1 | convolution fusion | flops 1610874880 | bytes 4194309 | tf_op jit(solution)/shard_map/while/body/eval_jaxpr/dot_general | solution.py:42
  247.7 3.3 %fusion.16 = f32[256,512]{1,0:T(8,128)S(1)} fusion(f32[2,1024,512]{2,1,0:T(8,128)S(1)} %get-tuple-element.347, f32[256,8192]{1,0:T(8,128)} %get-tuple-element.383, s32[]{:T(128)S(6)} %select_n.28, f32[256,512]{1,0:T(8,128)S(1)} %get-tuple-element.365, pred[]{:T(512)S(6)} %compare.3), kind=kOutput, calls=%fused_computation.8.clone.1 | convolution fusion | flops 1610874880 | bytes 4194309 | tf_op jit(solution)/shard_map/while/body/eval_jaxpr/dot_general | solution.py:39
  251.0 0.1 broadcast_add_fusion.2
  251.1 1.9 multiply_reduce_fusion.3
  253.0 3.3 %fusion.17 = f32[256,512]{1,0:T(8,128)S(1)} fusion(f32[2,1024,512]{2,1,0:T(8,128)S(1)} %get-tuple-element.347, f32[256,8192]{1,0:T(8,128)} %get-tuple-element.389, s32[]{:T(128)S(6)} %select_n.28, f32[256,512]{1,0:T(8,128)S(1)} %get-tuple-element.366, pred[]{:T(512)S(6)} %compare.3), kind=kOutput, calls=%fused_computation.9.clone.1 | convolution fusion | flops 1610874880 | bytes 4194309 | tf_op jit(solution)/shard_map/while/body/eval_jaxpr/dot_general | solution.py:42
  256.3 3.3 %fusion.16 = f32[256,512]{1,0:T(8,128)S(1)} fusion(f32[2,1024,512]{2,1,0:T(8,128)S(1)} %get-tuple-element.347, f32[256,8192]{1,0:T(8,128)} %get-tuple-element.383, s32[]{:T(128)S(6)} %select_n.28, f32[256,512]{1,0:T(8,128)S(1)} %get-tuple-element.365, pred[]{:T(512)S(6)} %compare.3), kind=kOutput, calls=%fused_computation.8.clone.1 | convolution fusion | flops 1610874880 | bytes 4194309 | tf_op jit(solution)/shard_map/while/body/eval_jaxpr/dot_general | solution.py:39
  259.6 0.1 broadcast_add_fusion.2
  259.6 1.9 multiply_reduce_fusion.3
  261.5 3.3 %fusion.17 = f32[256,512]{1,0:T(8,128)S(1)} fusion(f32[2,1024,512]{2,1,0:T(8,128)S(1)} %get-tuple-element.347, f32[256,8192]{1,0:T(8,128)} %get-tuple-element.389, s32[]{:T(128)S(6)} %select_n.28, f32[256,512]{1,0:T(8,128)S(1)} %get-tuple-element.366, pred[]{:T(512)S(6)} %compare.3), kind=kOutput, calls=%fused_computation.9.clone.1 | convolution fusion | flops 1610874880 | bytes 4194309 | tf_op jit(solution)/shard_map/while/body/eval_jaxpr/dot_general | solution.py:42
  264.8 3.3 %fusion.16 = f32[256,512]{1,0:T(8,128)S(1)} fusion(f32[2,1024,512]{2,1,0:T(8,128)S(1)} %get-tuple-element.347, f32[256,8192]{1,0:T(8,128)} %get-tuple-element.383, s32[]{:T(128)S(6)} %select_n.28, f32[256,512]{1,0:T(8,128)S(1)} %get-tuple-element.365, pred[]{:T(512)S(6)} %compare.3), kind=kOutput, calls=%fused_computation.8.clone.1 | convolution fusion | flops 1610874880 | bytes 4194309 | tf_op jit(solution)/shard_map/while/body/eval_jaxpr/dot_general | solution.py:39
  268.1 0.1 broadcast_add_fusion.2
  268.2 1.9 multiply_reduce_fusion.3
  270.1 3.3 %fusion.17 = f32[256,512]{1,0:T(8,128)S(1)} fusion(f32[2,1024,512]{2,1,0:T(8,128)S(1)} %get-tuple-element.347, f32[256,8192]{1,0:T(8,128)} %get-tuple-element.389, s32[]{:T(128)S(6)} %select_n.28, f32[256,512]{1,0:T(8,128)S(1)} %get-tuple-element.366, pred[]{:T(512)S(6)} %compare.3), kind=kOutput, calls=%fused_computation.9.clone.1 | convolution fusion | flops 1610874880 | bytes 4194309 | tf_op jit(solution)/shard_map/while/body/eval_jaxpr/dot_general | solution.py:42
  273.3 3.3 %fusion.16 = f32[256,512]{1,0:T(8,128)S(1)} fusion(f32[2,1024,512]{2,1,0:T(8,128)S(1)} %get-tuple-element.347, f32[256,8192]{1,0:T(8,128)} %get-tuple-element.383, s32[]{:T(128)S(6)} %select_n.28, f32[256,512]{1,0:T(8,128)S(1)} %get-tuple-element.365, pred[]{:T(512)S(6)} %compare.3), kind=kOutput, calls=%fused_computation.8.clone.1 | convolution fusion | flops 1610874880 | bytes 4194309 | tf_op jit(solution)/shard_map/while/body/eval_jaxpr/dot_general | solution.py:39
  276.6 0.1 broadcast_add_fusion.2
  276.7 1.9 multiply_reduce_fusion.3
  278.6 3.3 %fusion.17 = f32[256,512]{1,0:T(8,128)S(1)} fusion(f32[2,1024,512]{2,1,0:T(8,128)S(1)} %get-tuple-element.347, f32[256,8192]{1,0:T(8,128)} %get-tuple-element.389, s32[]{:T(128)S(6)} %select_n.28, f32[256,512]{1,0:T(8,128)S(1)} %get-tuple-element.366, pred[]{:T(512)S(6)} %compare.3), kind=kOutput, calls=%fused_computation.9.clone.1 | convolution fusion | flops 1610874880 | bytes 4194309 | tf_op jit(solution)/shard_map/while/body/eval_jaxpr/dot_general | solution.py:42
  281.9 3.3 %fusion.16 = f32[256,512]{1,0:T(8,128)S(1)} fusion(f32[2,1024,512]{2,1,0:T(8,128)S(1)} %get-tuple-element.347, f32[256,8192]{1,0:T(8,128)} %get-tuple-element.383, s32[]{:T(128)S(6)} %select_n.28, f32[256,512]{1,0:T(8,128)S(1)} %get-tuple-element.365, pred[]{:T(512)S(6)} %compare.3), kind=kOutput, calls=%fused_computation.8.clone.1 | convolution fusion | flops 1610874880 | bytes 4194309 | tf_op jit(solution)/shard_map/while/body/eval_jaxpr/dot_general | solution.py:39
  285.2 0.7 rsqrt_select_fusion
  285.8 0.1 multiply_bitcast_fusion.1
  286.0 1.1 multiply_reduce_fusion.1
  287.1 15.6 %psum.7 = f32[512]{0:T(512)S(1)} all-reduce(f32[512]{0:T(512)S(1)} %get-tuple-element.266), channel_id=1, replica_groups=mesh['row'=8,'col'=32] {'row'}, use_global_device_ids=true, to_apply=%region_4.5 | all-reduce | flops 512 | bytes 4096 | tf_op jit(solution)/shard_map/psum | solution.py:56
  302.7 0.6 broadcast_multiply_fusion
  (35 shorter events, 0.2 us)
Async XLA Ops:
  7.2 106.8 %all-gather.3.cloned.1.call-start = ((), (), s32[]{:S(2)}) async-start(), calls=%async_computation | async-start | bytes 8650752 | tf_op jit(solution)/shard_map/all_gather | solution.py:23
  7.9 209.0 %all-gather.5.cloned.1.call-start = ((), (), s32[]{:S(2)}) async-start(), calls=%async_computation.1 | async-start | bytes 8650752 | tf_op jit(solution)/shard_map/all_gather | solution.py:24
Sparse Core Ops, SparseCore 0:
  10.4 103.4 all-gather.2
  116.4 100.4 all-gather.4
where the time goes:
time: 311 us; the launch traced here: 310 us
  waiting for transfers between devices  127 us (41%)
  blocking collectives  96.3 us (31%)
  matrix products  52.1 us (17%)
  other arithmetic  19.7 us (6%)
  between operations  14.1 us (5%)
    all_gather x1, waiting for transfers between devices, local(): lax.all_gather(lower_panel, 'col', axis=1, tiled=True)  103 us
    all_gather x1, blocking collectives, local(): lax.all_gather(weighted, 'col', axis=1, tiled=True)  41.5 us
    all_gather x1, blocking collectives, local(): lax.all_gather(pole_values, 'col', axis=1, tiled=True)  39.2 us
    dot_general x8, matrix products, advance(): jnp.dot(window[0], basis_tile[0], precision=exact_mode, preferred_element...  26 us
    dot_general x8, matrix products, advance(): jnp.dot(window[1], basis_tile[1], precision=exact_mode, preferred_element...  26 us
    all_gather x1, waiting for transfers between devices, local(): lax.all_gather(upper_panel, 'col', axis=1, tiled=True)  23.1 us
    psum x1, blocking collectives, local(): lax.psum(partial_weight, 'row') / (2 * rows_here * lax.axis_size('row'))  15.6 us
    reduce_sum x8, other arithmetic, advance(): jnp.sum(cauchy * cauchy, axis=(0, 1))  15 us
  transfers between devices with their start and end apart: 2, of which 2 were waited for; matrix products, arithmetic and copies ran while one was open for 0% of the time, Pallas kernels for 0%

commit v1 on v0

--- a/solution.py
+++ b/solution.py
@@ -1,11 +1,26 @@
+import functools
 import math
 import jax
 import jax.numpy as jnp
 from jax import lax
 from jax.sharding import PartitionSpec as P
+from jax.lax import all_to_all, axis_size
 
 N1 = 8192
 exact_mode = lax.Precision.HIGHEST
+
+
+def files_prepare(m, mesh_ax):
+    aux = jnp.concatenate(
+        all_to_all(
+            jnp.stack([m] * axis_size(mesh_ax), axis=0), mesh_ax, split_axis=0, concat_axis=0
+        ),
+        axis=1,
+    )
+    return aux
+
+
+_define_trails = functools.partial(files_prepare, mesh_ax="col")
 
 
 def cauchy_block(pole_vals, weights, shift_vals):
@@ -20,7 +35,7 @@
     child_base = jnp.array([0, N1], jnp.int32)
     zeros_acc = jnp.zeros((rows_here, own_cols), jnp.float32)
     pieces = (
-        lax.all_gather(upper_panel, "col", axis=1, tiled=True),
+        _define_trails(upper_panel),
         lax.all_gather(lower_panel, "col", axis=1, tiled=True),
         lax.all_gather(pole_values, "col", axis=1, tiled=True),
         lax.all_gather(weighted, "col", axis=1, tiled=True),

time: 311 us -> 448 us (1.44)
  blocking collectives: 96.3 us -> 319 us
  waiting for transfers between devices: 127 us -> 0.68 us
  local copies, waits for them, and re-layouts: 0.02 us -> 14.2 us
  starting transfers between devices: 0.08 us -> 12.3 us
  other arithmetic: 19.7 us -> 27.5 us
  matrix products: 52.1 us -> 58.5 us
    all_gather x1, blocking collectives: 41.5 us -> 250 us  [local(): lax.all_gather(weighted, 'col', axis=1, tiled=True)]
    all_gather x1, waiting for transfers between devices: 103 us -> 0.01 us  [local(): lax.all_gather(lower_panel, 'col', axis=1, tiled=True)]
    all_gather x1 -> x0, waiting for transfers between devices: 23.1 us -> none  [local(): lax.all_gather(upper_panel, 'col', axis=1, tiled=True)]
    psum x1, blocking collectives: 15.6 us -> 32.6 us  [local(): lax.psum(partial_weight, 'row') / (2 * rows_here * lax.axis_size('row'))]
    all_to_all x0 -> x1, starting transfers between devices: none -> 12.3 us  [files_prepare(): all_to_all(jnp.stack([m] * axis_size(mesh_ax), axis=0), mesh_ax, split_ax...]
    reduce_sum x8, other arithmetic: 15 us -> 24.9 us  [advance(): jnp.sum(cauchy * cauchy, axis=(0, 1))]
    all_to_all x0 -> x1, local copies, waits for them, and re-layouts: none -> 8.94 us  [files_prepare(): all_to_all(jnp.stack([m] * axis_size(mesh_ax), axis=0), mesh_ax, split_ax...]
    dot_general x8, matrix products: 26 us -> 32.5 us  [advance(): jnp.dot(window[1], basis_tile[1], precision=exact_mode, preferred_element...]
  transfers between devices with their start and end apart: 2 -> 2, of which waited for: 2 -> 0; matrix products, arithmetic and copies ran while one was open for 0% -> 2% of each run, Pallas kernels for 0% -> 0%
where the time goes in v1:
time: 448 us; the launch traced here: 447 us
  blocking collectives  319 us (71%)
  matrix products  58.5 us (13%)
  other arithmetic  27.5 us (6%)
  local copies, waits for them, and re-layouts  14.2 us (3%)
  between operations  14.1 us (3%)
  starting transfers between devices  12.3 us (3%)
    all_gather x1, blocking collectives, local(): lax.all_gather(weighted, 'col', axis=1, tiled=True)  250 us
    all_gather x1, blocking collectives, local(): lax.all_gather(pole_values, 'col', axis=1, tiled=True)  36.8 us
    psum x1, blocking collectives, local(): lax.psum(partial_weight, 'row') / (2 * rows_here * lax.axis_size('row'))  32.6 us
    dot_general x8, matrix products, advance(): jnp.dot(window[1], basis_tile[1], precision=exact_mode, preferred_element...  32.5 us
    dot_general x8, matrix products, advance(): jnp.dot(window[0], basis_tile[0], precision=exact_mode, preferred_element...  26 us
    reduce_sum x8, other arithmetic, advance(): jnp.sum(cauchy * cauchy, axis=(0, 1))  24.9 us
    all_to_all x1, starting transfers between devices, files_prepare(): all_to_all(jnp.stack([m] * axis_size(mesh_ax), axis=0), mesh_ax, split_ax...  12.3 us
  transfers between devices with their start and end apart: 2, of which 0 were waited for; matrix products, arithmetic and copies ran while one was open for 2% of the time, Pallas kernels for 0%

profile of v1, /device:TPU:1, one launch (start us, length us, event | category | flops | bytes accessed | tf_op | source)
XLA Modules:
  0.0 446.9 jit_solution(10430833083388205625)
XLA Ops:
  7.2 5.1 %stack.8 = f32[32,256,256]{2,1,0:T(8,128)} broadcast(f32[256,256]{1,0:T(8,128)} %param.10), dimensions={1,2} | broadcast | bytes 8650752 | tf_op jit(solution)/shard_map/stack | solution.py:16
  12.3 0.0 copy-start.3
  12.3 0.0 copy-start.4
  12.3 0.0 copy-start.5
  12.3 0.0 copy-start.1
  12.3 12.3 %all-to-all-start = ((f32[32,256,256]{2,1,0:T(8,128)}), f32[32,256,256]{2,1,0:T(8,128)}, u32[]{:S(2)}, u32[]{:S(2)}) async-start(f32[32,256,256]{2,1,0:T(8,128)} %stack.8), calls=%async_computation | async-start | bytes 16777216 | tf_op jit(solution)/shard_map/all_to_all | solution.py:15
  24.6 0.0 all-gather.2.cloned.1.call-start
  24.6 0.7 all-gather.2.cloned.1.call-update
  25.4 0.0 copy-done.3
  25.4 0.0 copy-done.4
  25.4 249.6 %all_gather.9 = f32[2,8192]{1,0:T(2,128)S(1)} all-gather(f32[2,256]{1,0:T(2,128)S(1)} %convert_multiply_fusion), channel_id=1, replica_groups=mesh['row'=8,'col'=32] {'col'}, dimensions={1}, use_global_device_ids=true | all-gather | bytes 67584 | tf_op jit(solution)/shard_map/all_gather | solution.py:41
  275.0 0.0 copy-done.5
  275.0 36.8 %all_gather.10 = f32[2,8192]{1,0:T(2,128)S(1)} all-gather(f32[2,256]{1,0:T(2,128)S(1)} %copy-done.5), channel_id=1, replica_groups=mesh['row'=8,'col'=32] {'col'}, dimensions={1}, use_global_device_ids=true | all-gather | bytes 67584 | tf_op jit(solution)/shard_map/all_gather | solution.py:40
  311.9 0.0 copy-done.1
  311.9 0.0 copy-start.2
  311.9 0.0 all-to-all-done
  311.9 8.9 %copy.12 = f32[32,256,256]{1,2,0:T(8,128)} copy(f32[32,256,256]{2,1,0:T(8,128)} %all-to-all-done) | data formatting | bytes 16777216 | tf_op jit(solution)/shard_map/all_to_all | solution.py:15
  320.8 0.0 all-gather.2.cloned.1.call-done
  320.8 0.0 copy-done.2
  320.8 84.8 %while.18 = (s32[]{:T(128)}, f32[256,512]{1,0:T(8,128)S(1)}, f32[256,512]{1,0:T(8,128)S(1)}, f32[512]{0:T(512)S(1)}, f32[256,8192]{0,1:T(8,128)}, /*index=5*/pre...) while((s32[]{:T(128)}, f32[256,512]{1,0:T(8,128)S(1)}, ...), condition=%wide.region_2.3_spmd.clone, body=%wide.region_0.2_spmd.clone.sunk | while | flops 3229093376 | bytes 29446912 | solution.py:62
  320.9 0.1 broadcast_add_fusion.2
  320.9 3.1 multiply_reduce_fusion.3
  324.0 4.1 fusion.17
  328.1 0.0 copy-done
  328.1 3.3 fusion.16
  331.5 0.1 broadcast_add_fusion.2
  331.5 3.1 multiply_reduce_fusion.3
  334.6 4.1 fusion.17
  338.7 0.0 copy-done
  338.7 3.3 fusion.16
  342.1 0.1 broadcast_add_fusion.2
  342.1 3.1 multiply_reduce_fusion.3
  345.3 4.1 fusion.17
  349.3 0.0 copy-done
  349.3 3.3 fusion.16
  352.7 0.1 broadcast_add_fusion.2
  352.7 3.1 multiply_reduce_fusion.3
  355.9 4.1 fusion.17
  359.9 0.0 copy-done
  359.9 3.3 fusion.16
  363.3 0.1 broadcast_add_fusion.2
  363.3 3.1 multiply_reduce_fusion.3
  366.5 4.1 fusion.17
  370.5 0.0 copy-done
  370.5 3.3 fusion.16
  373.9 0.1 broadcast_add_fusion.2
  374.0 3.1 multiply_reduce_fusion.3
  377.1 4.1 fusion.17
  381.1 0.0 copy-done
  381.1 3.3 fusion.16
  384.5 0.1 broadcast_add_fusion.2
  384.6 3.1 multiply_reduce_fusion.3
  387.7 4.1 fusion.17
  391.7 0.0 copy-done
  391.7 3.3 fusion.16
  395.1 0.1 broadcast_add_fusion.2
  395.2 3.1 multiply_reduce_fusion.3
  398.3 4.1 fusion.17
  402.3 0.0 copy-done
  402.4 3.3 fusion.16
  405.7 0.1 multiply_bitcast_fusion.1
  405.8 1.1 multiply_reduce_fusion.1
  406.9 32.6 %psum.7 = f32[512]{0:T(512)S(1)} all-reduce(f32[512]{0:T(512)S(1)} %get-tuple-element.288), channel_id=1, replica_groups=mesh['row'=8,'col'=32] {'row'}, use_global_device_ids=true, to_apply=%region_4.5 | all-reduce | flops 512 | bytes 4096 | tf_op jit(solution)/shard_map/psum | solution.py:71
  439.5 0.6 broadcast_multiply_fusion
  (46 shorter events, 0.3 us)
Async XLA Ops:
  12.3 13.1 %copy-start.3 = (f32[2,256]{1,0:T(2,128)S(1)}, f32[2,256]{1,0:T(2,128)}, u32[]{:S(2)}) copy-start(f32[2,256]{1,0:T(2,128)} %param.13) | copy-start | bytes 6148
  12.3 13.1 %copy-start.4 = (s32[2,256]{1,0:T(2,128)S(1)}, s32[2,256]{1,0:T(2,128)}, u32[]{:S(2)}) copy-start(s32[2,256]{1,0:T(2,128)} %param.14) | copy-start | bytes 6148
  12.3 262.8 %copy-start.5 = (f32[2,256]{1,0:T(2,128)S(1)}, f32[2,256]{1,0:T(2,128)}, u32[]{:S(2)}) copy-start(f32[2,256]{1,0:T(2,128)} %param.12) | copy-start | bytes 6148
  12.3 299.6 %copy-start.1 = (s32[512]{0:T(512)S(1)}, s32[512]{0:T(512)}, u32[]{:S(2)}) copy-start(s32[512]{0:T(512)} %param.16) | copy-start | bytes 6148
  12.3 299.6 %all-to-all-start = ((f32[32,256,256]{2,1,0:T(8,128)}), f32[32,256,256]{2,1,0:T(8,128)}, u32[]{:S(2)}, u32[]{:S(2)}) async-start(f32[32,256,256]{2,1,0:T(8,128)} %stack.8), calls=%async_computation | async-start | bytes 16777216 | tf_op jit(solution)/shard_map/all_to_all | solution.py:15
  24.6 296.2 %all-gather.2.cloned.1.call-start = ((), (), s32[]{:S(2)}) async-start(), calls=%async_computation.1 | async-start | bytes 8650752 | tf_op jit(solution)/shard_map/all_gather | solution.py:39
  311.9 9.0 %copy-start.2 = (f32[512]{0:T(512)S(1)}, f32[512]{0:T(512)}, u32[]{:S(2)}) copy-start(f32[512]{0:T(512)} %param.15) | copy-start | bytes 6148
  324.0 4.1 copy-start
  334.6 4.1 copy-start
  345.3 4.1 copy-start
  355.9 4.1 copy-start
  366.5 4.1 copy-start
  377.1 4.1 copy-start
  387.7 4.1 copy-start
  398.3 4.1 copy-start
Sparse Core Ops, SparseCore 0:
  27.9 237.8 all-gather.1
